TPU v7x, 256 devices: a whole 4x4x8 slice. The times are simulated.
256 devices in a mesh: feat: 16 (over z, y_hi), ex: 16 (over y_lo, x, core).
Axes of the slice: x: 4, y: 4 (y_hi: 2, y_lo: 2; y = y_hi * 2 + y_lo), z: 8, core: 2. Of those that a mesh axis runs over, the one named last changes fastest.
Arguments:
- activations: bfloat16 [1024, 28672], P('ex', 'feat'), may hold values from -6 to 6
- out_grads: bfloat16 [1024, 8192], P('feat', 'ex'), may hold values from -6 to 6
- basis_in: bfloat16 [28672, 28672], P('feat', 'ex'), may hold values from -0.03125 to 0.03125
- basis_out: bfloat16 [8192, 8192], P('ex', 'feat'), may hold values from -0.0625 to 0.0625
Outputs:
- correction: float32 [8192, 28672], P('feat', 'ex')
All inputs are finite; a program needn't handle non-finite values.
Results may differ from a plain program's by a relative error of at most 0.0034.
Values may be sent and summed in bfloat16 or wider, within the bound.
A program may use at most 64 MiB of HBM per device.

v0:
```python
import jax
import jax.numpy as jnp
from jax import lax
from jax.sharding import PartitionSpec as P

SEQ_LEN = 256


def per_device(activations, out_grads, basis_in, basis_out):
    partial_in = jnp.dot(
        lax.all_gather(activations, "ex", axis=0, tiled=True),
        basis_in,
        preferred_element_type=jnp.float32,
    )
    rotated_in = lax.psum(partial_in, "feat").astype(jnp.bfloat16)
    grad_all = lax.all_gather(out_grads, "feat", axis=0, tiled=True)
    out_share = lax.psum_scatter(
        jnp.dot(grad_all, basis_out, preferred_element_type=jnp.float32),
        "ex",
        scatter_dimension=0,
        tiled=True,
    )
    rotated_out = lax.all_gather(out_share.astype(jnp.bfloat16), "ex", axis=0, tiled=True)
    tokens_all = rotated_in.shape[0]
    seq_count = tokens_all // SEQ_LEN
    in_blocks = rotated_in.reshape(seq_count, SEQ_LEN, rotated_in.shape[1])
    out_blocks = rotated_out.reshape(seq_count, SEQ_LEN, rotated_out.shape[1])
    per_seq = jnp.einsum("nto,nti->noi", out_blocks, in_blocks, preferred_element_type=jnp.float32)
    total = jnp.sum(per_seq * per_seq, axis=0)
    return total / jnp.float32(tokens_all)


def solution(mesh):
    return jax.shard_map(
        per_device,
        mesh=mesh,
        in_specs=(P("ex", "feat"), P("feat", "ex"), P("feat", "ex"), P("ex", "feat")),
        out_specs=P("feat", "ex"),
        check_vma=False,
    )
```

profile of v0, /device:TPU:16, one launch (start us, length us, event | category | flops | bytes accessed | tf_op | source)
XLA Modules:
  0.0 534.4 jit_solution(13047750849756554427)
XLA Ops:
  6.5 0.0 copy-start
  6.5 0.0 all-gather.4.cloned.1.call-start
  6.5 0.7 all-gather.4.cloned.1.call-update
  7.3 0.0 reduce-scatter.2.cloned.1.call-start
  7.3 81.7 %all-gather.4.cloned.1.call-done = bf16[1024,512]{1,0:T(8,128)(2,1)} async-done(((bf16[64,512]{1,0:T(8,128)(2,1)}), bf16[1024,512]{1,0:T(8,128)(2,1)}) %all-gather.4.cloned.1.call-update) | async-done | bytes 1048592 | tf_op jit(solution)/shard_map/all_gather | solution.py:16
  89.0 0.0 copy-done
  89.0 3.2 fusion
  92.2 0.0 reduce-scatter.2.cloned.1.call-update
  92.3 0.0 all-gather.8.cloned.1.call-start
  92.3 0.7 all-gather.8.cloned.1.call-update
  93.0 0.0 all-gather.6.cloned.1.call-start
  93.1 64.5 %reduce-scatter.2.cloned.1.call-done = f32[64,512]{1,0:T(8,128)} async-done(((f32[1024,512]{1,0:T(8,128)}), f32[64,512]{1,0:T(8,128)}) %reduce-scatter.2.cloned.1.call-update) | async-done | bytes 131088 | tf_op jit(solution)/shard_map/reduce_scatter | solution.py:17
  157.6 1.5 convert_element_type.6
  159.1 0.0 all-gather.6.cloned.1.call-update
  159.1 38.1 %all-gather.8.cloned.1.call-done = bf16[1024,1792]{1,0:T(8,128)(2,1)} async-done(((bf16[64,1792]{1,0:T(8,128)(2,1)}), bf16[1024,1792]{1,0:T(8,128)(2,1)}) %all-gather.8.cloned.1.call-update) | async-done | bytes 3670032 | tf_op jit(solution)/shard_map/all_gather | solution.py:11
  197.3 12.2 %fusion.1 = f32[1024,1792]{1,0:T(8,128)} fusion(bf16[1024,1792]{1,0:T(8,128)(2,1)} %all-gather.8.cloned.1.call-done, bf16[1792,1792]{1,0:T(8,128)(2,1)} %param.6), kind=kOutput, calls=%fused_computation.3 | convolution fusion | flops 6576668672 | bytes 17432576 | tf_op jit(solution)/shard_map/dot_general | solution.py:10
  209.5 311.6 %all-reduce.1 = bf16[1024,1792]{1,0:T(8,128)(2,1)} all-reduce(f32[1024,1792]{1,0:T(8,128)} %fusion.1), channel_id=1, replica_groups=mesh['feat'=16,'ex'=16] {'feat'}, use_global_device_ids=true, to_apply=%region_1.0 | all-reduce | flops 1835008 | bytes 11010048 | tf_op jit(solution)/shard_map/psum | solution.py:15
  521.0 0.0 all-gather.6.cloned.1.call-done
  521.0 4.8 multiply_reduce_fusion
  525.8 2.1 broadcast_multiply_fusion
Async XLA Ops:
  6.5 82.5 %copy-start = (bf16[512,512]{1,0:T(8,128)(2,1)S(1)}, bf16[512,512]{1,0:T(8,128)(2,1)}, u32[]{:S(2)}) copy-start(bf16[512,512]{1,0:T(8,128)(2,1)} %param.7) | copy-start | bytes 1572868
  6.5 82.5 %all-gather.4.cloned.1.call-start = ((), (), s32[]{:S(2)}) async-start(), calls=%async_computation.1 | async-start | bytes 1114112 | tf_op jit(solution)/shard_map/all_gather | solution.py:16
  7.3 150.3 %reduce-scatter.2.cloned.1.call-start = ((), (), s32[]{:S(2)}) async-start(), calls=%async_computation.2 | async-start | bytes 2228224 | tf_op jit(solution)/shard_map/reduce_scatter | solution.py:17
  92.3 105.0 %all-gather.8.cloned.1.call-start = ((), (), s32[]{:S(2)}) async-start(), calls=%async_computation.4 | async-start | bytes 3899392 | tf_op jit(solution)/shard_map/all_gather | solution.py:11
  93.0 428.0 %all-gather.6.cloned.1.call-start = ((), (), s32[]{:S(2)}) async-start(), calls=%async_computation.3 | async-start | bytes 1114112 | tf_op jit(solution)/shard_map/all_gather | solution.py:23
Sparse Core Ops, SparseCore 0:
  9.9 79.0 all-gather.3
  92.4 65.1 reduce-scatter.1
  159.4 37.8 all-gather.7
  199.0 45.0 all-gather.5
where the time goes:
time: 540 us; the launch traced here: 534 us
  blocking collectives  312 us (58%)
  waiting for transfers between devices  186 us (34%)
  matrix products  20.2 us (4%)
  between operations  13.1 us (2%)
    psum x1, blocking collectives, per_device(): rotated_in = lax.psum(partial_in, 'feat').astype(jnp.bfloat16)  312 us
    all_gather x1, waiting for transfers between devices, per_device(): grad_all = lax.all_gather(out_grads, 'feat', axis=0, tiled=True)  81.7 us
    reduce_scatter x1, waiting for transfers between devices, per_device(): lax.psum_scatter(jnp.dot(grad_all, basis_out, preferred_element_type=jnp....  64.5 us
    all_gather x1, waiting for transfers between devices, per_device(): lax.all_gather(activations, 'ex', axis=0, tiled=True)  38.1 us
    dot_general x1, matrix products, per_device(): jnp.dot(lax.all_gather(activations, 'ex', axis=0, tiled=True), basis_in,...  12.2 us
  transfers between devices with their start and end apart: 4, of which 3 were waited for; matrix products, arithmetic and copies ran while one was open for 3% of the time, Pallas kernels for 0%

commit v1 on v0

v1 whole, which is shorter than its diff:
```python
import functools

import jax
import jax.numpy as jnp
from jax import lax
from jax.experimental import pallas as pl
from jax.experimental.pallas import tpu as pltpu
from jax.sharding import PartitionSpec as P

SEQ_LEN = 256
BC = 256
MESH = pl.DeviceIdType.MESH
F32, BF16 = jnp.float32, jnp.bfloat16
NZ, NX = 8, 4
STOP = None


def kernel(sz, a_hbm, g_hbm, bi_hbm, bo_hbm, out_hbm, a_full, bi, part, sbuf, rbuf, tot, yrecv, rin, outv, g_full, bo,
           pout, sib, ro, rout, rout_t, a_ss, a_rs, gy_s, g_ss, g_rs, rs_ss, rs_rs, y_ss, y_rs, ag_ss, ag_rs,
           ob_s, oq_ss, oq_rs, ot_ss, ot_rs, of_ss, of_rs, lsem, out_sem):
    tk, nb = sz
    f, e = lax.axis_index("feat"), lax.axis_index("ex")
    z, yh = f // 2, f % 2
    ci, c = e // 2, e % 2
    yl, x = ci // NX, ci % NX
    yo, xm, xp, x2 = 1 - yl, (x + NX - 1) % NX, (x + 1) % NX, (x + 2) % NX
    t2 = 2 * tk

    def dev(z_=z, yh_=yh, yl_=yl, x_=x, c_=c):
        return {"feat": z_ * 2 + yh_, "ex": (yl_ * NX + x_) * 2 + c_}

    def send(src, dst, ss, rs, to):
        return pltpu.make_async_remote_copy(
            src_ref=src, dst_ref=dst, send_sem=ss, recv_sem=rs, device_id=to, device_id_type=MESH
        )

    zp, zm = dev(z_=(z + 1) % NZ), dev(z_=(z + NZ - 1) % NZ)
    sibling, ypair, yhpair = dev(c_=1 - c), dev(yl_=yo), dev(yh_=1 - yh)
    xpd, xmd = dev(x_=xp), dev(x_=xm)

    def chip(d):
        k = (ci + d) % (2 * NX)
        return k, {"feat": f, "ex": k * 2 + c}

    barrier = pltpu.get_barrier_semaphore()
    others = [zp, zm, sibling, yhpair] + [chip(d)[1] for d in range(1, 2 * NX)]
    for to in others:
        pl.semaphore_signal(barrier, inc=1, device_id=to, device_id_type=MESH)

    ld_bi = pltpu.make_async_copy(bi_hbm, bi, lsem.at[0])
    ld_bo = pltpu.make_async_copy(bo_hbm, bo, lsem.at[1])

    def rows(yl_, x_, c_=c, off=0, size=tk):
        return pl.ds(pl.multiple_of(((yl_ * NX + x_) * 2 + c_) * tk + off, tk // 2), size)

    ld_a = pltpu.make_async_copy(a_hbm, a_full.at[rows(yl, x)], lsem.at[2])
    frow = pl.ds(pl.multiple_of(f * tk, tk), tk)
    ld_g = pltpu.make_async_copy(g_hbm, g_full.at[frow], lsem.at[3])
    for ld in (ld_a, ld_g, ld_bo, ld_bi):
        ld.start()
    pl.semaphore_wait(barrier, len(others))

    hk = tk // 2
    a_out = [
        (rows(yl, x), ypair), (rows(yl, x), xpd), (rows(yl, x), xmd),
        (rows(yl, xm, size=hk), xpd), (rows(yl, xp, off=hk, size=hk), xmd),
        (rows(yo, x), xpd), (rows(yo, x), xmd), (rows(yl, x2), ypair),
    ]
    a_in = [rows(yo, x), rows(yl, xm), rows(yl, xp), rows(yl, x2, size=hk), rows(yl, x2, off=hk, size=hk),
            rows(yo, xm), rows(yo, xp), rows(yo, x2)]
    shards = [(yl, x), (yl, xm), (yl, xp), (yo, x), (yo, xm), (yo, xp), (yl, x2), (yo, x2)]
    for s in shards:
        a_out.append((rows(*s), sibling))
        a_in.append(rows(*s, c_=1 - c))

    def a_msg(i):
        r, to = a_out[i]
        src = a_hbm if i in (0, 1, 2, 8) else a_full.at[r]
        return send(src, a_full.at[r], a_ss.at[i], a_rs.at[i], to)

    def a_wait(i):
        r = a_full.at[a_in[i]]
        send(r, r, a_ss.at[i], a_rs.at[i], a_out[i][1]).wait_recv()

    def ag_region(ref, s, way, incoming):
        o = (z + NZ - s + (0 if incoming else 1)) if way == 0 else (z + s - (0 if incoming else 1))
        start = (o % NZ) * t2
        if s == 4:
            return ref.at[pl.ds(pl.multiple_of(start + way * tk, tk), tk)]
        return ref.at[pl.ds(pl.multiple_of(start, t2), t2)]

    def ag_send(ref, s, way, ss, rs):
        r = ag_region(ref, s, way, False)
        return send(r, r, ss.at[way, s - 1], rs.at[way, s - 1], zm if way else zp)

    def ag_wait(ref, s, way, ss, rs):
        r = ag_region(ref, s, way, True)
        send(r, r, ss.at[way, s - 1], rs.at[way, s - 1], zm if way else zp).wait_recv()

    gy = send(g_hbm, g_full.at[frow], gy_s.at[0], gy_s.at[1], yhpair)
    gy.start()
    for i in (0, 1, 2, 8):
        a_msg(i).start()
    orow = pl.ds(pl.multiple_of((z * 2 + 1 - yh) * tk, tk), tk)
    send(g_full.at[orow], g_full.at[orow], gy_s.at[0], gy_s.at[1], yhpair).wait_recv()
    ld_g.wait()

    def g_step(s):
        for way in (0, 1):
            if s > 1:
                ag_wait(g_full, s - 1, way, g_ss, g_rs)
            if s <= 4:
                ag_send(g_full, s, way, g_ss, g_rs).start()

    g_step(1)
    a_wait(1), a_msg(3).start(), a_msg(9).start()
    a_wait(2), a_msg(4).start(), a_msg(10).start()
    a_wait(0), a_msg(5).start(), a_msg(6).start(), a_msg(11).start()
    g_step(2)
    a_wait(3), a_wait(4), a_msg(7).start(), a_msg(14).start()
    g_step(3)
    a_wait(5), a_msg(12).start()
    a_wait(6), a_msg(13).start()
    g_step(4)
    a_wait(7), a_msg(15).start()
    ld_a.wait()
    for i in range(8, 16):
        a_wait(i)
    ld_bi.wait()

    def own(b, o):
        return part[b, pl.ds(pl.multiple_of((o % NZ) * t2, t2), t2), :]

    def rs_size(s):
        return pl.ds(0, tk if s == 1 else t2)

    def rs_copy(b, s, way):
        r = rs_size(s)
        return send(
            sbuf.at[b, way, s - 1, r], rbuf.at[b, way, s - 1, r], rs_ss.at[b, way, s - 1], rs_rs.at[b, way, s - 1],
            zm if way else zp,
        )

    def rs_first(b):
        start = ((z + 4) % NZ) * t2
        for way in (0, 1):
            r = pl.ds(pl.multiple_of(start + way * tk, tk), tk)
            sbuf[b, way, 0, rs_size(1), :] = part[b, r, :].astype(BF16)
            rs_copy(b, 1, way).start()

    def rs_next(b, s):
        for way in (0, 1):
            rs_copy(b, s - 1, way).wait_recv()
            mine = own(b, z + NZ - (5 - s) if way else z + (5 - s))
            if s == 2:
                got = rbuf[b, way, 0, rs_size(1), :].astype(F32)
                there = slice(way * tk, way * tk + tk)
                rest = slice((1 - way) * tk, (1 - way) * tk + tk)
                sbuf[b, way, 1, there, :] = (mine[there] + got).astype(BF16)
                sbuf[b, way, 1, rest, :] = mine[rest].astype(BF16)
            else:
                sbuf[b, way, s - 1] = (mine + rbuf[b, way, s - 2].astype(F32)).astype(BF16)
            rs_copy(b, s, way).start()

    def y_copy(b):
        return send(tot.at[b], yrecv.at[b], y_ss.at[b], y_rs.at[b], yhpair)

    def rs_last(b):
        for way in (0, 1):
            rs_copy(b, 4, way).wait_recv()
        tot[b] = own(b, z) + rbuf[b, 0, 3].astype(F32) + rbuf[b, 1, 3].astype(F32)
        y_copy(b).start()

    def ag_step(b, s):
        for way in (0, 1):
            if s > 1:
                ag_wait(rin.at[b], s - 1, way, ag_ss.at[b], ag_rs.at[b])
            if s <= 4:
                ag_send(rin.at[b], s, way, ag_ss.at[b], ag_rs.at[b]).start()

    def y_last(b):
        y_copy(b).wait_recv()
        rin[b, pl.ds(pl.multiple_of(z * t2, t2), t2), :] = (tot[b] + yrecv[b]).astype(BF16)
        ag_step(b, 1)

    def out_copy(b):
        cols = pl.ds(pl.multiple_of(b * BC, BC), BC)
        return pltpu.make_async_copy(outv.at[b], out_hbm.at[:, cols], out_sem.at[b])

    def correction(b):
        ag_step(b, 5)
        total = None
        for n in range(rout_t.shape[1] // SEQ_LEN):
            per_seq = jnp.dot(
                rout_t[:, n * SEQ_LEN : (n + 1) * SEQ_LEN],
                rin[b, n * SEQ_LEN : (n + 1) * SEQ_LEN, :],
                preferred_element_type=F32,
            )
            total = per_seq * per_seq if total is None else total + per_seq * per_seq
        outv[b] = total
        out_copy(b).start()

    ob = send(pout.at[1 - c], sib, ob_s.at[0], ob_s.at[1], sibling)

    def out_partial():
        g_step(5)
        ld_bo.wait()
        per = 4 * tk
        for m in range(g_full.shape[0] // per):
            val = jnp.dot(g_full[m * per : (m + 1) * per, :], bo[...], preferred_element_type=F32)
            for k in range(4):
                pout[k % 2, 2 * m + k // 2] = val[k * tk : (k + 1) * tk]
        ob.start()

    def oq_copy(d):
        k, to = chip(d)
        return send(pout.at[c, k], ro.at[ci], oq_ss.at[d], oq_rs.at[d], to)

    def out_pair():
        ob.wait_recv()
        for k in range(2 * NX):
            pout[c, k] = pout[c, k] + sib[k]
        for d in range(1, 2 * NX):
            oq_copy(d).start()

    def erow(k, c_):
        return pl.ds(pl.multiple_of((k * 2 + c_) * tk, tk), tk)

    def ot_copy(d):
        r = rout.at[erow(ci, c)]
        return send(r, r, ot_ss.at[d], ot_rs.at[d], chip(d)[1])

    def of_copy(d):
        r = rout.at[erow((ci + 2 * NX - d) % (2 * NX), c)]
        return send(r, r, of_ss.at[d], of_rs.at[d], sibling)

    def out_sum():
        total = pout[c, ci]
        for d in range(1, 2 * NX):
            k = (ci + 2 * NX - d) % (2 * NX)
            send(ro.at[k], ro.at[k], oq_ss.at[d], oq_rs.at[d], chip(d)[1]).wait_recv()
            total = total + ro[k]
        rout[erow(ci, c), :] = total.astype(BF16)
        for d in range(1, 2 * NX):
            ot_copy(d).start()
        of_copy(0).start()

    def out_forward():
        for d in range(1, 2 * NX):
            r = rout.at[erow((ci + 2 * NX - d) % (2 * NX), c)]
            send(r, r, ot_ss.at[d], ot_rs.at[d], chip(d)[1]).wait_recv()
            of_copy(d).start()

    def out_done():
        for d in range(2 * NX):
            r = rout.at[erow((ci + 2 * NX - d) % (2 * NX), 1 - c)]
            send(r, r, of_ss.at[d], of_rs.at[d], sibling).wait_recv()
        for m in range(rout.shape[0] // SEQ_LEN):
            rout_t[:, m * SEQ_LEN : (m + 1) * SEQ_LEN] = rout[m * SEQ_LEN : (m + 1) * SEQ_LEN, :].T

    out_phase = {2: out_partial, 3: out_pair, 5: out_sum, 7: out_forward, 8: out_done}

    def slot(t, carry):
        def block(lag, run):
            b = t - lag

            @pl.when((b >= 0) & (b < nb))
            def _():
                run(jnp.clip(b, 0, nb - 1))

        def product(b):
            cols = pl.ds(pl.multiple_of(b * BC, BC), BC)
            part[b] = jnp.dot(a_full[...], bi[:, cols], preferred_element_type=F32)
            rs_first(b)

        block(0, product)
        for lag in (1, 2, 3):
            block(lag, functools.partial(rs_next, s=lag + 1))
        block(4, rs_last)
        for at, run in out_phase.items():
            pl.when(t == at)(run)
        block(5, y_last)
        for lag in (6, 7, 8):
            block(lag, functools.partial(ag_step, s=lag - 4))
        block(9, correction)
        return carry

    lax.fori_loop(0, nb + 9, slot, 0)

    for i in range(16):
        a_msg(i).wait_send()
    gy.wait_send()
    ob.wait_send()
    for s in range(1, 5):
        for way in (0, 1):
            ag_send(g_full, s, way, g_ss, g_rs).wait_send()
    for d in range(2 * NX):
        of_copy(d).wait_send()
        if d:
            oq_copy(d).wait_send()
            ot_copy(d).wait_send()

    def drain(b, carry):
        for s in range(1, 5):
            for way in (0, 1):
                rs_copy(b, s, way).wait_send()
                ag_send(rin.at[b], s, way, ag_ss.at[b], ag_rs.at[b]).wait_send()
        y_copy(b).wait_send()
        out_copy(b).wait()
        return carry

    lax.fori_loop(0, nb, drain, 0)


def per_device(activations, out_grads, basis_in, basis_out):
    tk, kin = activations.shape
    kout, nout = basis_out.shape
    nin = basis_in.shape[1]
    nb, tokens = nin // BC, tk * 16
    dma, vmem = pltpu.SemaphoreType.DMA, pltpu.VMEM
    squares = pl.pallas_call(
        functools.partial(kernel, (tk, nb)),
        out_shape=jax.ShapeDtypeStruct((nout, nin), F32),
        in_specs=[pl.BlockSpec(memory_space=pl.ANY)] * 4,
        out_specs=pl.BlockSpec(memory_space=pl.ANY),
        scratch_shapes=[
            vmem((tokens, kin), BF16),
            vmem((kin, nin), BF16),
            vmem((nb, tokens, BC), F32),
            vmem((nb, 2, 4, 2 * tk, BC), BF16),
            vmem((nb, 2, 4, 2 * tk, BC), BF16),
            vmem((nb, 2 * tk, BC), F32),
            vmem((nb, 2 * tk, BC), F32),
            vmem((nb, tokens, BC), BF16),
            vmem((nb, nout, BC), F32),
            vmem((tokens, kout), BF16),
            vmem((kout, nout), BF16),
            vmem((2, 8, tk, nout), F32),
            vmem((8, tk, nout), F32),
            vmem((8, tk, nout), F32),
            vmem((tokens, nout), BF16),
            vmem((nout, tokens), BF16),
            dma((16,)), dma((16,)), dma((2,)), dma((2, 4)), dma((2, 4)),
            dma((nb, 2, 4)), dma((nb, 2, 4)), dma((nb,)), dma((nb,)), dma((nb, 2, 4)), dma((nb, 2, 4)),
            dma((2,)), dma((8,)), dma((8,)), dma((8,)), dma((8,)), dma((8,)), dma((8,)), dma((4,)), dma((nb,)),
        ],
        compiler_params=pltpu.CompilerParams(
            collective_id=0, has_side_effects=True, vmem_limit_bytes=60 * 1024 * 1024
        ),
    )(activations, out_grads, basis_in, basis_out)
    return squares / jnp.float32(tokens)


def solution(mesh):
    return jax.shard_map(
        per_device,
        mesh=mesh,
        in_specs=(P("ex", "feat"), P("feat", "ex"), P("feat", "ex"), P("ex", "feat")),
        out_specs=P("feat", "ex"),
        check_vma=False,
    )
```

time: 540 us -> 122 us (0.23); the launches traced: 534 us -> 122 us
  blocking collectives: 312 us -> 0 us
  waiting for transfers between devices: 186 us -> 0 us
  Pallas kernels: 0 us -> 118 us
  matrix products: 20.2 us -> 0 us
  between operations: 13.1 us -> 0.01 us
    psum x1 -> x0, blocking collectives: 312 us -> none  [per_device(): rotated_in = lax.psum(partial_in, 'feat').astype(jnp.bfloat16)]
    all_gather x3 -> x0, waiting for transfers between devices: 120 us -> none  [the longest x1 81.7 us: per_device(): grad_all = lax.all_gather(out_grads, 'feat', axis=0, tiled=True)]
    pallas_call x0 -> x1, Pallas kernels: none -> 118 us  [per_device(): pl.pallas_call(functools.partial(kernel, (tk, nb)), out_shape=jax.ShapeDt...]
    reduce_scatter x1 -> x0, waiting for transfers between devices: 64.5 us -> none  [per_device(): lax.psum_scatter(jnp.dot(grad_all, basis_out, preferred_element_type=jnp....]
    dot_general x3 -> x0, matrix products: 20.2 us -> none  [the longest x1 12.2 us: per_device(): jnp.dot(lax.all_gather(activations, 'ex', axis=0, tiled=True), basis_in,...]
  transfers between devices with their start and end apart: 4 -> 0, of which waited for: 3 -> 0; matrix products, arithmetic and copies ran while one was open for 3% -> 0% of each run, Pallas kernels for 0% -> 0%
where the time goes in v1:
time: 122 us
  Pallas kernels  118 us (97%)
  other arithmetic  4.11 us (3%)
    pallas_call x1, Pallas kernels, per_device(): pl.pallas_call(functools.partial(kernel, (tk, nb)), out_shape=jax.ShapeDt...  118 us
    div x1, other arithmetic, per_device(): return squares / jnp.float32(tokens)  4.11 us

profile of v1, /device:TPU:16, one launch (start us, length us, event | category | flops | bytes accessed | tf_op | source)
XLA Modules:
  0.0 122.3 jit_solution(5198242182022865610)
XLA Ops:
  0.0 118.2 %shard_map.46 = f32[512,1792]{1,0:T(8,128)} custom-call(bf16[64,1792]{1,0:T(8,128)(2,1)} %a_hbm.1, bf16[64,512]{1,0:T(8,128)(2,1)} %g_hbm.1, bf16[1792,1792]{1,0:T(8,128)(2,1)} %bi_hbm.1, bf16[512,512]{1,0:T(8,128)(2,1)} %bo_hbm.1), custom_call_target="tpu_custom_call" | custom-call | tf_op jit(solution)/shard_map/pallas_call | solution.py:321
  118.2 4.1 %broadcast_multiply_fusion = f32[512,1792]{1,0:T(8,128)} fusion(f32[512,1792]{1,0:T(8,128)} %shard_map.46), kind=kLoop, calls=%fused_computation | loop fusion | flops 917504 | bytes 7340032 | tf_op jit(solution)/shard_map/div | solution.py:351

commit v2 on v0

v2 whole, which is shorter than its diff:
```python
import functools

import jax
import jax.numpy as jnp
from jax import lax
from jax.experimental import pallas as pl
from jax.experimental.pallas import tpu as pltpu
from jax.sharding import PartitionSpec as P

SEQ_LEN = 256
BC = 256
NG = 1
MESH = pl.DeviceIdType.MESH
F32, BF16 = jnp.float32, jnp.bfloat16
NZ, NX = 8, 4
Y_ITEMS = (0, 1, 2, 4, 5)
ORDER = (
    (0, 0, -1), (2, 0, 1), (1, 0, 0), (2, 0, 2), (0, 0, 1), (0, 0, 2), (2, 0, 3), (0, 0, 0), (2, 1, 1), (2, 0, 4),
    (0, 0, 4), (2, 1, 2), (2, 1, 3), (0, 0, 5), (0, 0, 6), (0, 0, 7), (2, 1, 4), (0, 0, 8), (4, 0, 0), (4, 1, 0), (4, 2, 0),
    (3, 1, 0), (4, 0, 1), (4, 3, 0), (4, 0, 2), (3, 2, 0), (4, 1, 1), (4, 3, 1), (4, 4, 0), (4, 1, 2), (4, 0, 3), (4, 3, 2),
    (4, 2, 1), (4, 5, 0), (4, 0, 4), (4, 2, 2), (4, 1, 3), (4, 6, 0), (4, 0, 5), (4, 4, 1), (4, 1, 4), (3, 3, 0), (4, 2, 3),
    (4, 0, 6), (4, 6, 1), (4, 4, 2), (4, 1, 5), (4, 5, 1), (4, 2, 4), (4, 0, 7), (4, 3, 3), (4, 6, 2), (3, 4, 0), (4, 4, 3),
    (4, 1, 6), (4, 5, 2), (4, 2, 5), (4, 0, 8), (4, 3, 4), (4, 6, 3), (4, 4, 4), (3, 5, 0), (4, 1, 7), (4, 5, 3), (4, 2, 6),
    (4, 0, 9), (4, 6, 4), (4, 4, 5), (4, 1, 8), (4, 3, 5), (4, 5, 4), (4, 2, 7), (3, 6, 0), (4, 4, 6), (4, 1, 9), (3, 7, 0),
    (4, 3, 6), (4, 2, 8), (4, 0, 10), (5, 0, 0), (4, 4, 7), (4, 5, 5), (4, 6, 5), (4, 3, 7), (4, 2, 9), (4, 4, 8),
    (4, 5, 6), (4, 6, 6), (4, 1, 10), (5, 1, 0), (4, 3, 8), (4, 4, 9), (4, 5, 7), (4, 6, 7), (4, 2, 10), (5, 2, 0),
    (4, 5, 8), (4, 3, 9), (5, 3, 0), (4, 6, 8), (4, 4, 10), (4, 5, 9), (5, 4, 0), (4, 6, 9), (5, 6, 0), (4, 5, 10),
    (5, 5, 0),
)


def kernel(dims, a_hbm, g_hbm, bi_hbm, bo_hbm, out, a_full, bi, part, sbuf, rbuf, ysend, yrecv, tot, ytot, rin, g_full, bo,
           pout, sib, ro, oy, rout, rout_t, a_ss, a_rs, gy_s, g_ss, g_rs, rs_ss, rs_rs, y_ss, y_rs, ag_ss, ag_rs, fy_ss, fy_rs,
           ob_s, oy_s, oq_ss, oq_rs, ot_ss, ot_rs, of_ss, of_rs, lsem):
    tg, nb = dims
    tk = tg // NG
    ni = nb * NG
    f, e = lax.axis_index("feat"), lax.axis_index("ex")
    z, yh = f // 2, f % 2
    ci, c = e // 2, e % 2
    yl, x = ci // NX, ci % NX
    yo, xm, xp, x2 = 1 - yl, (x + NX - 1) % NX, (x + 1) % NX, (x + 2) % NX
    t2 = 2 * tk

    def dev(z_=z, yh_=yh, yl_=yl, x_=x, c_=c):
        return {"feat": z_ * 2 + yh_, "ex": (yl_ * NX + x_) * 2 + c_}

    def send(src, dst, ss, rs, to):
        return pltpu.make_async_remote_copy(
            src_ref=src, dst_ref=dst, send_sem=ss, recv_sem=rs, device_id=to, device_id_type=MESH
        )

    zp, zm = dev(z_=(z + 1) % NZ), dev(z_=(z + NZ - 1) % NZ)
    zdev = (zp, zm)
    sibling, ypair, yhpair = dev(c_=1 - c), dev(yl_=yo), dev(yh_=1 - yh)
    xpd, xmd = dev(x_=xp), dev(x_=xm)

    barrier = pltpu.get_barrier_semaphore()
    others = [zp, zm, sibling, ypair, yhpair, xpd, xmd, dev(x_=x2)]
    for to in others:
        pl.semaphore_signal(barrier, inc=1, device_id=to, device_id_type=MESH)

    def rows(yl_, x_, c_=c, off=0, size=tk):
        return pl.ds(pl.multiple_of(((yl_ * NX + x_) * 2 + c_) * tk + off, tk // 2), size)

    def half(ref, n, way):
        return ref.at[pl.ds(way * (n // 2), n // 2)]

    ld_bi = pltpu.make_async_copy(bi_hbm, bi, lsem.at[0])
    ld_bo = pltpu.make_async_copy(bo_hbm, bo, lsem.at[1])
    ld_g = pltpu.make_async_copy(g_hbm, g_full.at[z, yh], lsem.at[2])
    ld_a = [
        pltpu.make_async_copy(a_hbm.at[pl.ds(h * tk, tk)], a_full.at[h, rows(yl, x)], lsem.at[3 + h]) for h in range(NG)
    ]
    for ld in (*ld_a, ld_g, ld_bo, ld_bi):
        ld.start()
    pl.semaphore_wait(barrier, len(others))

    hk = tk // 2
    a_out = [
        (rows(yl, x), ypair), (rows(yl, x), xpd), (rows(yl, x), xmd),
        (rows(yl, xm, size=hk), xpd), (rows(yl, xp, off=hk, size=hk), xmd),
        (rows(yo, x), xpd), (rows(yo, x), xmd), (rows(yl, x2), ypair),
    ]
    a_in = [rows(yo, x), rows(yl, xm), rows(yl, xp), rows(yl, x2, size=hk), rows(yl, x2, off=hk, size=hk),
            rows(yo, xm), rows(yo, xp), rows(yo, x2)]
    for s in [(yl, x), (yl, xm), (yl, xp), (yo, x), (yo, xm), (yo, xp), (yl, x2), (yo, x2)]:
        a_out.append((rows(*s), sibling))
        a_in.append(rows(*s, c_=1 - c))

    def a_msg(h, i):
        r, to = a_out[i]
        src = a_hbm.at[pl.ds(h * tk, tk)] if i in (0, 1, 2, 8) else a_full.at[h, r]
        return send(src, a_full.at[h, r], a_ss.at[h, i], a_rs.at[h, i], to)

    def a_wait(h, i, *then):
        r = a_full.at[h, a_in[i]]
        send(r, r, a_ss.at[h, i], a_rs.at[h, i], a_out[i][1]).wait_recv()
        for k in then:
            a_msg(h, k).start()

    def a_first(h):
        for i in (1, 2, 0, 8):
            a_msg(h, i).start()

    def a_done(h):
        ld_a[h].wait()
        for i in range(8, 16):
            a_wait(h, i)

    def ag_region(view, n, s, way, incoming):
        o = (z + NZ - s + (0 if incoming else 1)) if way == 0 else (z + s - (0 if incoming else 1))
        r = view(o % NZ)
        return half(r, n, way) if s == 4 else r

    def ag_copy(view, n, s, way, ss, rs, incoming=False):
        r = ag_region(view, n, s, way, incoming)
        return send(r, r, ss.at[way, s - 1], rs.at[way, s - 1], zdev[way])

    def ag_wait(view, n, s, way, ss, rs):
        ag_copy(view, n, s, way, ss, rs, True).wait_recv()

    def g_args(k):
        j = yh if k == 0 else 1 - yh
        return (lambda o: g_full.at[o, j]), tg, g_ss.at[k], g_rs.at[k]

    def g_copy(k, s, way):
        view, n, ss, rs = g_args(k)
        if k == 0 and s == 1:
            return send(g_hbm, view(z), ss.at[way, 0], rs.at[way, 0], zdev[way])
        return ag_copy(view, n, s, way, ss, rs)

    def g_step(k, s):
        view, n, ss, rs = g_args(k)
        for way in (0, 1):
            if s > 1:
                ag_wait(view, n, s - 1, way, ss, rs)
            if s <= 4:
                g_copy(k, s, way).start()

    gy = send(g_hbm, g_full.at[z, yh], gy_s.at[0], gy_s.at[1], yhpair)

    def is_y(i):
        return functools.reduce(jnp.logical_or, [i == k for k in Y_ITEMS])

    def zsize(kind):
        return t2 if kind == 0 else tk

    def mine(kind, i, o):
        if kind == 0:
            return part[i, o % NZ]
        return part[i, o % NZ, pl.ds(pl.multiple_of(yh * tk, tk), tk), :]

    def rs_copy(kind, i, s, way):
        n = zsize(kind)
        r = pl.ds(0, n // 2 if s == 1 else n)
        return send(
            sbuf.at[i, way, s - 1, r], rbuf.at[i, way, s - 1, r], rs_ss.at[i, way, s - 1], rs_rs.at[i, way, s - 1], zdev[way]
        )

    def rs_first(kind, i):
        n = zsize(kind)
        whole = mine(kind, i, z + 4)
        for way in (0, 1):
            sbuf[i, way, 0, pl.ds(0, n // 2), :] = whole[way * (n // 2) : (way + 1) * (n // 2)].astype(BF16)
            rs_copy(kind, i, 1, way).start()

    def rs_next(kind, i, s):
        n = zsize(kind)
        m = n // 2
        for way in (0, 1):
            rs_copy(kind, i, s - 1, way).wait_recv()
            own = mine(kind, i, z + NZ - (5 - s) if way else z + (5 - s))
            if s == 2:
                got = rbuf[i, way, 0, pl.ds(0, m), :].astype(F32)
                sbuf[i, way, 1, pl.ds(way * m, m), :] = (own[way * m : (way + 1) * m] + got).astype(BF16)
                sbuf[i, way, 1, pl.ds((1 - way) * m, m), :] = own[(1 - way) * m : (2 - way) * m].astype(BF16)
            else:
                got = rbuf[i, way, s - 2, pl.ds(0, n), :].astype(F32)
                sbuf[i, way, s - 1, pl.ds(0, n), :] = (own + got).astype(BF16)
            rs_copy(kind, i, s, way).start()

    def rs_last(kind, i):
        n = zsize(kind)
        for way in (0, 1):
            rs_copy(kind, i, 4, way).wait_recv()
        got = [rbuf[i, way, 3, pl.ds(0, n), :].astype(F32) for way in (0, 1)]
        return mine(kind, i, z) + got[0] + got[1]

    def view(kind, i):
        if kind == 0:
            return lambda o: rin.at[i, o]
        return lambda o: rin.at[i, o, pl.ds(pl.multiple_of(yh * tk, tk), tk)]

    def ag_step(kind, i, s):
        n = zsize(kind)
        for way in (0, 1):
            if s > 1:
                ag_wait(view(kind, i), n, s - 1, way, ag_ss.at[i], ag_rs.at[i])
            if s <= 4:
                ag_copy(view(kind, i), n, s, way, ag_ss.at[i], ag_rs.at[i]).start()
            if kind == 1 and s > 1:
                fy_copy(i, s - 1, way).start()
        if kind == 1 and s == 1:
            fy_copy(i, 0, 0).start()

    def y_copy(i):
        return send(tot.at[i], ytot.at[i], y_ss.at[i], y_rs.at[i], yhpair)

    def z_last(i):
        tot[i] = rs_last(0, i)
        y_copy(i).start()

    def z_sum(i):
        y_copy(i).wait_recv()
        rin[i, z] = (tot[i] + ytot[i]).astype(BF16)
        ag_step(0, i, 1)

    def yp_copy(i):
        return send(ysend.at[i], yrecv.at[i], y_ss.at[i], y_rs.at[i], yhpair)

    def y_start(i):
        other = pl.ds(pl.multiple_of((1 - yh) * tk, tk), tk)
        for o in range(NZ):
            ysend[i, o] = part[i, o, other, :].astype(BF16)
        yp_copy(i).start()

    def y_sum(i):
        yp_copy(i).wait_recv()
        own = pl.ds(pl.multiple_of(yh * tk, tk), tk)
        for o in range(NZ):
            part[i, o, own, :] = part[i, o, own, :] + yrecv[i, o].astype(F32)
        rs_first(1, i)

    def y_last(i):
        rin[i, z, pl.ds(pl.multiple_of(yh * tk, tk), tk), :] = rs_last(1, i).astype(BF16)
        ag_step(1, i, 1)

    def fy_region(i, s, way, j):
        r = rin.at[i, ((z + s) if way else (z + NZ - s)) % NZ, pl.ds(pl.multiple_of(j * tk, tk), tk)]
        return half(r, tk, way) if s == 4 else r

    def fy_copy(i, s, way, incoming=False):
        r = fy_region(i, s, way, 1 - yh if incoming else yh)
        return send(r, r, fy_ss.at[i, s, way], fy_rs.at[i, s, way], yhpair)

    fy_all = [(0, 0)] + [(s, way) for s in range(1, 5) for way in (0, 1)]

    def y_done(i):
        for s, way in fy_all:
            fy_copy(i, s, way, True).wait_recv()

    def correction(b):
        cols = pl.ds(pl.multiple_of(b * BC, BC), BC)
        total = None
        spans = 2 * SEQ_LEN // (tg * 2)
        for n in range(rout_t.shape[1] // SEQ_LEN):
            parts = [
                rin[h * nb + b, n * (spans // 2) + k] for h in range(NG) for k in range(spans // 2)
            ]
            per_seq = jnp.dot(
                rout_t[:, n * SEQ_LEN : (n + 1) * SEQ_LEN],
                jnp.concatenate(parts, axis=0),
                preferred_element_type=F32,
            )
            total = per_seq * per_seq if total is None else total + per_seq * per_seq
        out[:, cols] = total

    ob = send(pout.at[1 - c], sib, ob_s.at[0], ob_s.at[1], sibling)

    def out_partial():
        g_step(0, 5)
        g_step(1, 5)
        ld_g.wait()
        ld_bo.wait()
        for m in range(NZ // 2):
            grads = g_full[2 * m : 2 * m + 2].reshape(4 * tg, g_full.shape[3])
            val = jnp.dot(grads, bo[...], preferred_element_type=F32)
            for k in range(4):
                at = 2 * m + k // 2
                pout[k % 2, at // NX, at % NX] = val[k * tg : (k + 1) * tg]
        ob.start()

    def xplace(d):
        return (x + NX + d) % NX

    def oq_copy(d):
        return send(pout.at[c, :, xplace(d)], ro.at[x], oq_ss.at[d], oq_rs.at[d], dev(x_=xplace(d)))

    def out_pair():
        ob.wait_recv()
        for row in (0, 1):
            for k in range(NX):
                pout[c, row, k] = pout[c, row, k] + sib[row, k]
        for d in range(1, NX):
            oq_copy(d).start()

    def oy_copy():
        return send(pout.at[c, yo, x], oy, oy_s.at[0], oy_s.at[1], ypair)

    def out_row():
        for d in range(1, NX):
            r = ro.at[xplace(-d)]
            send(r, r, oq_ss.at[d], oq_rs.at[d], xpd).wait_recv()
        for row in (0, 1):
            total = pout[c, row, x]
            for d in range(1, NX):
                total = total + ro[xplace(-d), row]
            pout[c, row, x] = total
        oy_copy().start()

    def piece(r, d, c_=c):
        row = yo if r else yl
        return rout.at[pl.ds(pl.multiple_of(((row * NX + xplace(-d)) * 2 + c_) * tg, tg), tg)]

    def ot_copy(r, d):
        src = piece(r, 0)
        return send(src, src, ot_ss.at[r, d], ot_rs.at[r, d], dev(x_=xplace(d)) if d else ypair)

    def ot_wait(r, d):
        dst = piece(r, d) if d else piece(1, 0)
        send(dst, dst, ot_ss.at[r, d], ot_rs.at[r, d], xpd).wait_recv()

    def of_copy(r, d, c_=c):
        src = piece(r, d, c_)
        return send(src, src, of_ss.at[r, d], of_rs.at[r, d], sibling)

    def out_sum():
        oy_copy().wait_recv()
        rout[pl.ds(pl.multiple_of(e * tg, tg), tg), :] = (pout[c, yl, x] + oy[...]).astype(BF16)
        for d in range(NX):
            ot_copy(0, d).start()
        of_copy(0, 0).start()

    def out_forward():
        ot_wait(0, 0)
        of_copy(1, 0).start()
        for d in range(1, NX):
            ot_copy(1, d).start()
        for d in range(1, NX):
            ot_wait(0, d)
            of_copy(0, d).start()

    def out_forward2():
        for d in range(1, NX):
            ot_wait(1, d)
            of_copy(1, d).start()

    def out_done():
        for r in (0, 1):
            for d in range(NX):
                of_copy(r, d, 1 - c).wait_recv()
        for n in range(rout.shape[0] // SEQ_LEN):
            seq = rout[n * SEQ_LEN : (n + 1) * SEQ_LEN, :]
            parts = [
                seq[k * tg + h * tk : k * tg + (h + 1) * tk] for h in range(NG) for k in range(SEQ_LEN // tg)
            ]
            rout_t[:, n * SEQ_LEN : (n + 1) * SEQ_LEN] = jnp.concatenate(parts, axis=0).T

    def product(i):
        b = i % nb
        if (4, i, 0) == first_item:
            ld_bi.wait()
        val = jnp.dot(a_full[i // nb], bi[:, b * BC : (b + 1) * BC], preferred_element_type=F32)
        part[i] = val.reshape(NZ, t2, BC)

    def activations(h, k):
        if k == -1:
            a_first(h)
        elif k == 4:
            a_wait(h, 3)
            a_wait(h, 4, 7, 14)
        elif k == 8:
            a_done(h)
        else:
            a_wait(h, k, *{1: (3, 9), 2: (4, 10), 0: (5, 6, 11), 5: (12,), 6: (13,), 7: (15,)}[k])

    def gradients(k, s):
        if (k, s) == (1, 1):
            r = g_full.at[z, 1 - yh]
            send(r, r, gy_s.at[0], gy_s.at[1], yhpair).wait_recv()
        g_step(k, s)

    def stage(i, k):
        if i in Y_ITEMS:
            if k == 0:
                product(i)
                y_start(i)
            elif k == 1:
                y_sum(i)
            elif k < 5:
                rs_next(1, i, k)
            elif k == 5:
                y_last(i)
            elif k < 10:
                ag_step(1, i, k - 4)
            else:
                y_done(i)
        elif k == 0:
            product(i)
            rs_first(0, i)
        elif k < 4:
            rs_next(0, i, k + 1)
        elif k == 4:
            z_last(i)
        elif k == 5:
            z_sum(i)
        else:
            ag_step(0, i, k - 4)

    out_phases = (out_partial, out_pair, out_row, out_sum, out_forward, out_forward2, out_done)
    first_item = next(op for op in ORDER if op[0] == 4)
    for op, p, q in ORDER:
        if op == 0:
            activations(p, q)
        elif op == 1:
            gy.start()
        elif op == 2:
            gradients(p, q)
        elif op == 3:
            out_phases[p - 1]()
        elif op == 4:
            stage(p, q)
        else:
            correction(p)

    gy.wait_send()
    ob.wait_send()
    for h in range(NG):
        for i in range(16):
            a_msg(h, i).wait_send()
    for k in (0, 1):
        for s in range(1, 5):
            for way in (0, 1):
                g_copy(k, s, way).wait_send()
    oy_copy().wait_send()
    for d in range(NX):
        for r in (0, 1):
            of_copy(r, d).wait_send()
            if d or r == 0:
                ot_copy(r, d).wait_send()
        if d:
            oq_copy(d).wait_send()

    def drain(i, carry):
        for kind in (0, 1):

            @pl.when(is_y(i) == (kind == 1))
            def _():
                for s in range(1, 5):
                    for way in (0, 1):
                        rs_copy(kind, i, s, way).wait_send()
                        ag_copy(view(kind, i), zsize(kind), s, way, ag_ss.at[i], ag_rs.at[i]).wait_send()
                if kind == 0:
                    y_copy(i).wait_send()
                else:
                    yp_copy(i).wait_send()
                    for s, way in fy_all:
                        fy_copy(i, s, way).wait_send()

        return carry

    lax.fori_loop(0, ni, drain, 0)


def per_device(activations, out_grads, basis_in, basis_out):
    tg, kin = activations.shape
    kout, nout = basis_out.shape
    nin = basis_in.shape[1]
    nb, tokens = nin // BC, tg * 16
    tk, ni = tg // NG, nb * NG
    dma, vmem = pltpu.SemaphoreType.DMA, pltpu.VMEM
    squares = pl.pallas_call(
        functools.partial(kernel, (tg, nb)),
        out_shape=jax.ShapeDtypeStruct((nout, nin), F32),
        in_specs=[pl.BlockSpec(memory_space=pl.ANY)] * 4,
        out_specs=pl.BlockSpec(memory_space=pltpu.VMEM),
        scratch_shapes=[
            vmem((NG, tokens // NG, kin), BF16),
            vmem((kin, nin), BF16),
            vmem((ni, NZ, 2 * tk, BC), F32),
            vmem((ni, 2, 4, 2 * tk, BC), BF16),
            vmem((ni, 2, 4, 2 * tk, BC), BF16),
            vmem((ni, NZ, tk, BC), BF16),
            vmem((ni, NZ, tk, BC), BF16),
            vmem((ni, 2 * tk, BC), F32),
            vmem((ni, 2 * tk, BC), F32),
            vmem((ni, NZ, 2 * tk, BC), BF16),
            vmem((NZ, 2, tg, kout), BF16),
            vmem((kout, nout), BF16),
            vmem((2, 2, NX, tg, nout), F32),
            vmem((2, NX, tg, nout), F32),
            vmem((NX, 2, tg, nout), F32),
            vmem((tg, nout), F32),
            vmem((tokens, nout), BF16),
            vmem((nout, tokens), BF16),
            dma((NG, 16)), dma((NG, 16)), dma((2,)), dma((2, 2, 4)), dma((2, 2, 4)),
            dma((ni, 2, 4)), dma((ni, 2, 4)), dma((ni,)), dma((ni,)), dma((ni, 2, 4)), dma((ni, 2, 4)),
            dma((ni, 5, 2)), dma((ni, 5, 2)),
            dma((2,)), dma((2,)), dma((NX,)), dma((NX,)), dma((2, NX)), dma((2, NX)), dma((2, NX)), dma((2, NX)), dma((3 + NG,)),
        ],
        compiler_params=pltpu.CompilerParams(
            collective_id=0, has_side_effects=True, vmem_limit_bytes=60 * 1024 * 1024
        ),
    )(activations, out_grads, basis_in, basis_out)
    return squares / jnp.float32(tokens)


def solution(mesh):
    return jax.shard_map(
        per_device,
        mesh=mesh,
        in_specs=(P("ex", "feat"), P("feat", "ex"), P("feat", "ex"), P("ex", "feat")),
        out_specs=P("feat", "ex"),
        check_vma=False,
    )
```

time: 540 us -> 111 us (0.21)
  blocking collectives: 312 us -> 0 us
  waiting for transfers between devices: 186 us -> 0 us
  Pallas kernels: 0 us -> 106 us
  matrix products: 20.2 us -> 0 us
  between operations: 13.1 us -> 0.01 us
    psum x1 -> x0, blocking collectives: 312 us -> none  [per_device(): rotated_in = lax.psum(partial_in, 'feat').astype(jnp.bfloat16)]
    all_gather x3 -> x0, waiting for transfers between devices: 120 us -> none  [the longest x1 81.7 us: per_device(): grad_all = lax.all_gather(out_grads, 'feat', axis=0, tiled=True)]
    pallas_call x0 -> x1, Pallas kernels: none -> 106 us  [per_device(): pl.pallas_call(functools.partial(kernel, (tg, nb)), out_shape=jax.ShapeDt...]
    reduce_scatter x1 -> x0, waiting for transfers between devices: 64.5 us -> none  [per_device(): lax.psum_scatter(jnp.dot(grad_all, basis_out, preferred_element_type=jnp....]
    dot_general x3 -> x0, matrix products: 20.2 us -> none  [the longest x1 12.2 us: per_device(): jnp.dot(lax.all_gather(activations, 'ex', axis=0, tiled=True), basis_in,...]
  transfers between devices with their start and end apart: 4 -> 0, of which waited for: 3 -> 0; matrix products, arithmetic and copies ran while one was open for 3% -> 0% of each run, Pallas kernels for 0% -> 0%
where the time goes in v2:
time: 111 us; the launch traced here: 110 us
  Pallas kernels  106 us (95%)
  other arithmetic  4.11 us (4%)
    pallas_call x1, Pallas kernels, per_device(): pl.pallas_call(functools.partial(kernel, (tg, nb)), out_shape=jax.ShapeDt...  106 us
    div x1, other arithmetic, per_device(): return squares / jnp.float32(tokens)  4.11 us

profile of v2, /device:TPU:16, one launch (start us, length us, event | category | flops | bytes accessed | tf_op | source)
XLA Modules:
  0.0 110.2 jit_solution(11606381489681587453)
XLA Ops:
  0.0 106.1 %shard_map.46 = f32[512,1792]{1,0:T(8,128)} custom-call(bf16[64,1792]{1,0:T(8,128)(2,1)} %a_hbm.1, bf16[64,512]{1,0:T(8,128)(2,1)} %g_hbm.1, bf16[1792,1792]{1,0:T(8,128)(2,1)} %bi_hbm.1, bf16[512,512]{1,0:T(8,128)(2,1)} %bo_hbm.1), custom_call_target="tpu_custom_call" | custom-call | tf_op jit(solution)/shard_map/pallas_call | solution.py:473
  106.1 4.1 %broadcast_multiply_fusion = f32[512,1792]{1,0:T(8,128)} fusion(f32[512,1792]{1,0:T(8,128)} %shard_map.46), kind=kLoop, calls=%fused_computation | loop fusion | flops 917504 | bytes 7340032 | tf_op jit(solution)/shard_map/div | solution.py:506

commit v3 on v2

--- a/solution.py
+++ b/solution.py
@@ -13,25 +13,25 @@
 MESH = pl.DeviceIdType.MESH
 F32, BF16 = jnp.float32, jnp.bfloat16
 NZ, NX = 8, 4
-Y_ITEMS = (0, 1, 2, 4, 5)
+Y_ITEMS = (1, 2, 3, 5, 6)
 ORDER = (
     (0, 0, -1), (2, 0, 1), (1, 0, 0), (2, 0, 2), (0, 0, 1), (0, 0, 2), (2, 0, 3), (0, 0, 0), (2, 1, 1), (2, 0, 4),
-    (0, 0, 4), (2, 1, 2), (2, 1, 3), (0, 0, 5), (0, 0, 6), (0, 0, 7), (2, 1, 4), (0, 0, 8), (4, 0, 0), (4, 1, 0), (4, 2, 0),
-    (3, 1, 0), (4, 0, 1), (4, 3, 0), (4, 0, 2), (3, 2, 0), (4, 1, 1), (4, 3, 1), (4, 4, 0), (4, 1, 2), (4, 0, 3), (4, 3, 2),
-    (4, 2, 1), (4, 5, 0), (4, 0, 4), (4, 2, 2), (4, 1, 3), (4, 6, 0), (4, 0, 5), (4, 4, 1), (4, 1, 4), (3, 3, 0), (4, 2, 3),
-    (4, 0, 6), (4, 6, 1), (4, 4, 2), (4, 1, 5), (4, 5, 1), (4, 2, 4), (4, 0, 7), (4, 3, 3), (4, 6, 2), (3, 4, 0), (4, 4, 3),
-    (4, 1, 6), (4, 5, 2), (4, 2, 5), (4, 0, 8), (4, 3, 4), (4, 6, 3), (4, 4, 4), (3, 5, 0), (4, 1, 7), (4, 5, 3), (4, 2, 6),
-    (4, 0, 9), (4, 6, 4), (4, 4, 5), (4, 1, 8), (4, 3, 5), (4, 5, 4), (4, 2, 7), (3, 6, 0), (4, 4, 6), (4, 1, 9), (3, 7, 0),
-    (4, 3, 6), (4, 2, 8), (4, 0, 10), (5, 0, 0), (4, 4, 7), (4, 5, 5), (4, 6, 5), (4, 3, 7), (4, 2, 9), (4, 4, 8),
-    (4, 5, 6), (4, 6, 6), (4, 1, 10), (5, 1, 0), (4, 3, 8), (4, 4, 9), (4, 5, 7), (4, 6, 7), (4, 2, 10), (5, 2, 0),
-    (4, 5, 8), (4, 3, 9), (5, 3, 0), (4, 6, 8), (4, 4, 10), (4, 5, 9), (5, 4, 0), (4, 6, 9), (5, 6, 0), (4, 5, 10),
-    (5, 5, 0),
+    (0, 0, 4), (2, 1, 2), (2, 1, 3), (0, 0, 5), (0, 0, 6), (0, 0, 7), (2, 1, 4), (0, 0, 8), (4, 6, 0), (3, 1, 0), (4, 5, 0),
+    (4, 4, 0), (4, 6, 1), (3, 2, 0), (4, 3, 0), (4, 6, 2), (4, 4, 1), (4, 2, 0), (4, 6, 3), (4, 5, 1), (4, 4, 2), (4, 1, 0),
+    (4, 5, 2), (4, 3, 1), (4, 4, 3), (4, 6, 4), (4, 0, 0), (4, 3, 2), (4, 5, 3), (3, 3, 0), (4, 6, 5), (4, 2, 1), (4, 0, 1),
+    (4, 3, 3), (4, 5, 4), (4, 4, 4), (4, 6, 6), (4, 2, 2), (4, 0, 2), (4, 1, 1), (4, 3, 4), (4, 5, 5), (4, 6, 7), (4, 2, 3),
+    (3, 4, 0), (4, 0, 3), (4, 1, 2), (4, 3, 5), (4, 4, 5), (4, 5, 6), (4, 6, 8), (4, 2, 4), (4, 0, 4), (4, 1, 3), (3, 5, 0),
+    (4, 3, 6), (4, 4, 6), (4, 5, 7), (4, 6, 9), (4, 2, 5), (4, 1, 4), (4, 3, 7), (4, 0, 5), (4, 4, 7), (3, 6, 0), (4, 5, 8),
+    (4, 2, 6), (4, 1, 5), (3, 7, 0), (4, 3, 8), (4, 0, 6), (4, 6, 10), (5, 6, 0), (4, 4, 8), (4, 5, 9), (4, 2, 7),
+    (4, 1, 6), (4, 3, 9), (4, 0, 7), (4, 4, 9), (5, 4, 0), (4, 2, 8), (4, 1, 7), (4, 5, 10), (5, 5, 0), (4, 0, 8),
+    (4, 2, 9), (4, 3, 10), (4, 1, 8), (5, 3, 0), (4, 0, 9), (5, 0, 0), (4, 1, 9), (4, 2, 10), (5, 2, 0), (4, 1, 10),
+    (5, 1, 0),
 )
 
 
-def kernel(dims, a_hbm, g_hbm, bi_hbm, bo_hbm, out, a_full, bi, part, sbuf, rbuf, ysend, yrecv, tot, ytot, rin, g_full, bo,
+def kernel(dims, a_hbm, g_hbm, bi_hbm, bo_hbm, out, a_full, bi, part, sbuf, rbuf, ysend, yrecv, tot, zsend, ytot, rin, g_full, bo,
            pout, sib, ro, oy, rout, rout_t, a_ss, a_rs, gy_s, g_ss, g_rs, rs_ss, rs_rs, y_ss, y_rs, ag_ss, ag_rs, fy_ss, fy_rs,
-           ob_s, oy_s, oq_ss, oq_rs, ot_ss, ot_rs, of_ss, of_rs, lsem):
+           ob_s, oy_s, oq_ss, oq_rs, ot_ss, ot_rs, of_ss, of_rs, lsem, out_sem, outv):
     tg, nb = dims
     tk = tg // NG
     ni = nb * NG
@@ -149,7 +149,8 @@
     def mine(kind, i, o):
         if kind == 0:
             return part[i, o % NZ]
-        return part[i, o % NZ, pl.ds(pl.multiple_of(yh * tk, tk), tk), :]
+        own = part[i, o % NZ, pl.ds(pl.multiple_of(yh * tk, tk), tk), :]
+        return own + yrecv[i, o % NZ].astype(F32)
 
     def rs_copy(kind, i, s, way):
         n = zsize(kind)
@@ -205,15 +206,17 @@
             fy_copy(i, 0, 0).start()
 
     def y_copy(i):
-        return send(tot.at[i], ytot.at[i], y_ss.at[i], y_rs.at[i], yhpair)
+        return send(zsend.at[i], ytot.at[i], y_ss.at[i], y_rs.at[i], yhpair)
 
     def z_last(i):
-        tot[i] = rs_last(0, i)
+        total = rs_last(0, i)
+        tot[i] = total
+        zsend[i] = total.astype(BF16)
         y_copy(i).start()
 
     def z_sum(i):
         y_copy(i).wait_recv()
-        rin[i, z] = (tot[i] + ytot[i]).astype(BF16)
+        rin[i, z] = (tot[i] + ytot[i].astype(F32)).astype(BF16)
         ag_step(0, i, 1)
 
     def yp_copy(i):
@@ -227,9 +230,6 @@
 
     def y_sum(i):
         yp_copy(i).wait_recv()
-        own = pl.ds(pl.multiple_of(yh * tk, tk), tk)
-        for o in range(NZ):
-            part[i, o, own, :] = part[i, o, own, :] + yrecv[i, o].astype(F32)
         rs_first(1, i)
 
     def y_last(i):
@@ -250,8 +250,10 @@
         for s, way in fy_all:
             fy_copy(i, s, way, True).wait_recv()
 
+    def out_copy(b):
+        return pltpu.make_async_copy(outv.at[b], out.at[b], out_sem.at[b])
+
     def correction(b):
-        cols = pl.ds(pl.multiple_of(b * BC, BC), BC)
         total = None
         spans = 2 * SEQ_LEN // (tg * 2)
         for n in range(rout_t.shape[1] // SEQ_LEN):
@@ -264,7 +266,8 @@
                 preferred_element_type=F32,
             )
             total = per_seq * per_seq if total is None else total + per_seq * per_seq
-        out[:, cols] = total
+        outv[b] = total / F32(SEQ_LEN * (rout_t.shape[1] // SEQ_LEN))
+        out_copy(b).start()
 
     ob = send(pout.at[1 - c], sib, ob_s.at[0], ob_s.at[1], sibling)
 
@@ -461,6 +464,21 @@
         return carry
 
     lax.fori_loop(0, ni, drain, 0)
+    for b in range(nb):
+        out_copy(b).wait()
+
+
+def store(blocks, out, held, in_sem, out_sem):
+    nb = blocks.shape[0]
+    into = [pltpu.make_async_copy(blocks.at[b], held.at[b], in_sem.at[b]) for b in range(nb)]
+    back = [pltpu.make_async_copy(held.at[b], out.at[:, pl.ds(b * BC, BC)], out_sem.at[b]) for b in range(nb)]
+    for copy in into:
+        copy.start()
+    for b in range(nb):
+        into[b].wait()
+        back[b].start()
+    for copy in back:
+        copy.wait()
 
 
 def per_device(activations, out_grads, basis_in, basis_out):
@@ -470,11 +488,11 @@
     nb, tokens = nin // BC, tg * 16
     tk, ni = tg // NG, nb * NG
     dma, vmem = pltpu.SemaphoreType.DMA, pltpu.VMEM
-    squares = pl.pallas_call(
+    corrected = pl.pallas_call(
         functools.partial(kernel, (tg, nb)),
-        out_shape=jax.ShapeDtypeStruct((nout, nin), F32),
+        out_shape=jax.ShapeDtypeStruct((nb, nout, BC), F32),
         in_specs=[pl.BlockSpec(memory_space=pl.ANY)] * 4,
-        out_specs=pl.BlockSpec(memory_space=pltpu.VMEM),
+        out_specs=pl.BlockSpec(memory_space=pltpu.HBM),
         scratch_shapes=[
             vmem((NG, tokens // NG, kin), BF16),
             vmem((kin, nin), BF16),
@@ -484,7 +502,8 @@
             vmem((ni, NZ, tk, BC), BF16),
             vmem((ni, NZ, tk, BC), BF16),
             vmem((ni, 2 * tk, BC), F32),
-            vmem((ni, 2 * tk, BC), F32),
+            vmem((ni, 2 * tk, BC), BF16),
+            vmem((ni, 2 * tk, BC), BF16),
             vmem((ni, NZ, 2 * tk, BC), BF16),
             vmem((NZ, 2, tg, kout), BF16),
             vmem((kout, nout), BF16),
@@ -497,13 +516,20 @@
             dma((NG, 16)), dma((NG, 16)), dma((2,)), dma((2, 2, 4)), dma((2, 2, 4)),
             dma((ni, 2, 4)), dma((ni, 2, 4)), dma((ni,)), dma((ni,)), dma((ni, 2, 4)), dma((ni, 2, 4)),
             dma((ni, 5, 2)), dma((ni, 5, 2)),
-            dma((2,)), dma((2,)), dma((NX,)), dma((NX,)), dma((2, NX)), dma((2, NX)), dma((2, NX)), dma((2, NX)), dma((3 + NG,)),
+            dma((2,)), dma((2,)), dma((NX,)), dma((NX,)), dma((2, NX)), dma((2, NX)), dma((2, NX)), dma((2, NX)), dma((3 + NG,)), dma((nb,)),
+            vmem((nb, nout, BC), F32),
         ],
         compiler_params=pltpu.CompilerParams(
-            collective_id=0, has_side_effects=True, vmem_limit_bytes=60 * 1024 * 1024
+            collective_id=0, has_side_effects=True, vmem_limit_bytes=58 * 1024 * 1024
         ),
     )(activations, out_grads, basis_in, basis_out)
-    return squares / jnp.float32(tokens)
+    return pl.pallas_call(
+        store,
+        out_shape=jax.ShapeDtypeStruct((nout, nin), F32),
+        in_specs=[pl.BlockSpec(memory_space=pltpu.HBM)],
+        out_specs=pl.BlockSpec(memory_space=pltpu.HBM),
+        scratch_shapes=[vmem((nb, nout, BC), F32), dma((nb,)), dma((nb,))],
+    )(corrected)
 
 
 def solution(mesh):

time: 111 us -> 107 us (0.964)
  other arithmetic: 4.11 us -> 0 us
    div x1 -> x0, other arithmetic: 4.11 us -> none  [per_device(): return squares / jnp.float32(tokens)]
    pallas_call x1, Pallas kernels: 106 us -> 102 us  [per_device(): pl.pallas_call(functools.partial(kernel, (tg, nb)), out_shape=jax.ShapeDt...]
    pallas_call x0 -> x1, Pallas kernels: none -> 3.02 us  [per_device(): pl.pallas_call(store, out_shape=jax.ShapeDtypeStruct((nout, nin), F32), i...]
where the time goes in v3:
time: 107 us; the launch traced here: 105 us
  Pallas kernels  105 us (98%)
    pallas_call x1, Pallas kernels, per_device(): pl.pallas_call(functools.partial(kernel, (tg, nb)), out_shape=jax.ShapeDt...  102 us
    pallas_call x1, Pallas kernels, per_device(): pl.pallas_call(store, out_shape=jax.ShapeDtypeStruct((nout, nin), F32), i...  3.02 us

profile of v3, /device:TPU:16, one launch (start us, length us, event | category | flops | bytes accessed | tf_op | source)
XLA Modules:
  0.0 105.5 jit_solution(16840696558343260178)
XLA Ops:
  0.0 102.4 %shard_map.46.blocks = f32[7,512,256]{2,1,0:T(8,128)} custom-call(bf16[64,1792]{1,0:T(8,128)(2,1)} %a_hbm.1, bf16[64,512]{1,0:T(8,128)(2,1)} %g_hbm.1, bf16[1792,1792]{1,0:T(8,128)(2,1)} %bi_hbm.1, bf16[512,512]{1,0:T(8,128)(2,1)} %bo_hbm.1), custom_call_target="tpu_custom_call" | custom-call | tf_op jit(solution)/shard_map/pallas_call | solution.py:491
  102.5 3.0 %shard_map.47 = f32[512,1792]{1,0:T(8,128)} custom-call(f32[7,512,256]{2,1,0:T(8,128)} %shard_map.46.blocks), custom_call_target="tpu_custom_call" | custom-call | tf_op jit(solution)/shard_map/pallas_call | solution.py:526

commit v4 on v3

--- a/solution.py
+++ b/solution.py
@@ -13,18 +13,18 @@
 MESH = pl.DeviceIdType.MESH
 F32, BF16 = jnp.float32, jnp.bfloat16
 NZ, NX = 8, 4
-Y_ITEMS = (1, 2, 3, 5, 6)
+Y_ITEMS = (1, 2, 4, 5, 6)
 ORDER = (
-    (0, 0, -1), (2, 0, 1), (1, 0, 0), (2, 0, 2), (0, 0, 1), (0, 0, 2), (2, 0, 3), (0, 0, 0), (2, 1, 1), (2, 0, 4),
-    (0, 0, 4), (2, 1, 2), (2, 1, 3), (0, 0, 5), (0, 0, 6), (0, 0, 7), (2, 1, 4), (0, 0, 8), (4, 6, 0), (3, 1, 0), (4, 5, 0),
-    (4, 4, 0), (4, 6, 1), (3, 2, 0), (4, 3, 0), (4, 6, 2), (4, 4, 1), (4, 2, 0), (4, 6, 3), (4, 5, 1), (4, 4, 2), (4, 1, 0),
-    (4, 5, 2), (4, 3, 1), (4, 4, 3), (4, 6, 4), (4, 0, 0), (4, 3, 2), (4, 5, 3), (3, 3, 0), (4, 6, 5), (4, 2, 1), (4, 0, 1),
-    (4, 3, 3), (4, 5, 4), (4, 4, 4), (4, 6, 6), (4, 2, 2), (4, 0, 2), (4, 1, 1), (4, 3, 4), (4, 5, 5), (4, 6, 7), (4, 2, 3),
-    (3, 4, 0), (4, 0, 3), (4, 1, 2), (4, 3, 5), (4, 4, 5), (4, 5, 6), (4, 6, 8), (4, 2, 4), (4, 0, 4), (4, 1, 3), (3, 5, 0),
-    (4, 3, 6), (4, 4, 6), (4, 5, 7), (4, 6, 9), (4, 2, 5), (4, 1, 4), (4, 3, 7), (4, 0, 5), (4, 4, 7), (3, 6, 0), (4, 5, 8),
-    (4, 2, 6), (4, 1, 5), (3, 7, 0), (4, 3, 8), (4, 0, 6), (4, 6, 10), (5, 6, 0), (4, 4, 8), (4, 5, 9), (4, 2, 7),
-    (4, 1, 6), (4, 3, 9), (4, 0, 7), (4, 4, 9), (5, 4, 0), (4, 2, 8), (4, 1, 7), (4, 5, 10), (5, 5, 0), (4, 0, 8),
-    (4, 2, 9), (4, 3, 10), (4, 1, 8), (5, 3, 0), (4, 0, 9), (5, 0, 0), (4, 1, 9), (4, 2, 10), (5, 2, 0), (4, 1, 10),
+    (0, 0, -1), (1, 0, 0), (2, 0, 1), (2, 0, 2), (0, 0, 1), (0, 0, 2), (0, 0, 0), (2, 0, 3), (2, 1, 1), (2, 0, 4),
+    (0, 0, 4), (2, 1, 2), (2, 1, 3), (0, 0, 5), (0, 0, 6), (0, 0, 7), (2, 1, 4), (0, 0, 8), (4, 6, 0), (4, 5, 0), (3, 1, 0),
+    (4, 4, 0), (4, 6, 1), (3, 2, 0), (4, 3, 0), (4, 6, 2), (4, 5, 1), (4, 2, 0), (4, 5, 2), (4, 3, 1), (4, 6, 3), (4, 1, 0),
+    (4, 3, 2), (4, 4, 1), (4, 6, 4), (4, 5, 3), (4, 0, 0), (4, 4, 2), (4, 6, 5), (3, 3, 0), (4, 2, 1), (4, 5, 4), (4, 0, 1),
+    (4, 6, 6), (4, 4, 3), (4, 2, 2), (4, 1, 1), (4, 5, 5), (4, 3, 3), (4, 0, 2), (4, 6, 7), (3, 4, 0), (4, 4, 4), (4, 1, 2),
+    (4, 2, 3), (4, 5, 6), (4, 3, 4), (4, 0, 3), (4, 6, 8), (4, 4, 5), (3, 5, 0), (4, 1, 3), (4, 2, 4), (4, 3, 5), (4, 5, 7),
+    (4, 0, 4), (4, 6, 9), (4, 4, 6), (4, 1, 4), (4, 2, 5), (3, 6, 0), (4, 3, 6), (4, 5, 8), (4, 4, 7), (4, 0, 5), (3, 7, 0),
+    (4, 1, 5), (4, 2, 6), (4, 4, 8), (4, 6, 10), (4, 3, 7), (4, 5, 9), (5, 6, 0), (4, 1, 6), (4, 0, 6), (4, 2, 7),
+    (4, 4, 9), (4, 3, 8), (4, 1, 7), (4, 5, 10), (4, 0, 7), (5, 5, 0), (4, 2, 8), (4, 3, 9), (4, 1, 8), (5, 3, 0),
+    (4, 0, 8), (4, 4, 10), (4, 2, 9), (4, 1, 9), (5, 4, 0), (4, 0, 9), (5, 0, 0), (4, 2, 10), (5, 2, 0), (4, 1, 10),
     (5, 1, 0),
 )
 

time: 107 us -> 108 us (level)
  Pallas kernels: 105 us -> 107 us
    pallas_call x1, Pallas kernels: 102 us -> 104 us  [per_device(): pl.pallas_call(functools.partial(kernel, (tg, nb)), out_shape=jax.ShapeDt...]
where the time goes in v4:
time: 108 us; the launch traced here: 107 us
  Pallas kernels  107 us (99%)
    pallas_call x1, Pallas kernels, per_device(): pl.pallas_call(functools.partial(kernel, (tg, nb)), out_shape=jax.ShapeDt...  104 us
    pallas_call x1, Pallas kernels, per_device(): pl.pallas_call(store, out_shape=jax.ShapeDtypeStruct((nout, nin), F32), i...  3.02 us

profile of v4, /device:TPU:16, one launch (start us, length us, event | category | flops | bytes accessed | tf_op | source)
XLA Modules:
  0.0 107.3 jit_solution(11558273444133620514)
XLA Ops:
  0.0 104.2 %shard_map.46.blocks = f32[7,512,256]{2,1,0:T(8,128)} custom-call(bf16[64,1792]{1,0:T(8,128)(2,1)} %a_hbm.1, bf16[64,512]{1,0:T(8,128)(2,1)} %g_hbm.1, bf16[1792,1792]{1,0:T(8,128)(2,1)} %bi_hbm.1, bf16[512,512]{1,0:T(8,128)(2,1)} %bo_hbm.1), custom_call_target="tpu_custom_call" | custom-call | tf_op jit(solution)/shard_map/pallas_call | solution.py:491
  104.3 3.0 %shard_map.47 = f32[512,1792]{1,0:T(8,128)} custom-call(f32[7,512,256]{2,1,0:T(8,128)} %shard_map.46.blocks), custom_call_target="tpu_custom_call" | custom-call | tf_op jit(solution)/shard_map/pallas_call | solution.py:526
